TPU v7x, 128 devices: a whole 4x4x4 slice. The times are simulated.
128 devices in a mesh: box: 32 (over y, z, core), tx: 4 (over x).
Axes of the slice: x: 4, y: 4, z: 4, core: 2. Of those that a mesh axis runs over, the one named last changes fastest.
Arguments:
- bank: bfloat16 [512, 1024, 1024], P('box', 'tx'), may hold values from -6 to 6
- pick: int32 [64], replicated, may hold values from 0 to 1023, as said below
- slot_box: int32 [512], replicated, may hold values from 0 to 511, each once
- leaf_factor: bfloat16 [512, 512, 128], P('box'), may hold values from -0.1875 to 0.1875
- self_factor: bfloat16 [9, 512, 64, 128], P(None, 'box'), may hold values from -0.375 to 0.375
- cross_factor: bfloat16 [9, 512, 64, 128], P(None, 'box'), may hold values from -0.375 to 0.375
- target_factor: bfloat16 [512, 64, 4096], P('box'), may hold values from -0.5 to 0.5
Outputs:
- field: bfloat16 [512, 64, 4096], P('box', 'tx')
Inputs may be any that keep to these rules, and one draw needn't show every extreme that they name: `pick`: distinct stored transmitters. `slot_box`: each box once.
All inputs are finite; a program needn't handle non-finite values.
Results may differ from a plain program's by a relative error of at most 0.023.
Values may be sent and summed in bfloat16 or wider, within the bound.
A program may use at most 128 MiB of HBM per device.

v0:
```python
import jax
import jax.numpy as jnp
from jax import lax
from jax.sharding import PartitionSpec as P


def partner_2(block, axis, bit):
    count = lax.axis_size(axis)
    route = []
    for low in range(count):
        high = low | 1 << bit
        if high != low and high < count:
            route += [(low, high), (high, low)]
    return lax.ppermute(block, axis, route)


def complex_times(values, matrix):
    inner = matrix.shape[-2]
    half = matrix.shape[-1] // 2
    first = jnp.einsum(
        "brn,bnk->brk", values[..., :inner], matrix, preferred_element_type=jnp.float32
    )
    second = jnp.einsum(
        "brn,bnk->brk", values[..., inner:], matrix, preferred_element_type=jnp.float32
    )
    return jnp.concatenate(
        [first[..., :half] - second[..., half:], first[..., half:] + second[..., :half]], axis=-1
    )


def per_device(bank, pick, slot_box, leaf_factor, self_factor, cross_factor, target_factor):
    box_dev = bank.shape[0]
    bank_dev = bank.shape[1]
    tx_index = lax.axis_index("tx")
    local_pick = pick - tx_index * bank_dev
    chooser = (local_pick[:, None] == jnp.arange(bank_dev, dtype=jnp.int32)[None, :]).astype(
        jnp.bfloat16
    )
    picked = jnp.einsum("pj,bju->bpu", chooser, bank, preferred_element_type=jnp.float32)
    owned = lax.psum_scatter(picked.astype(jnp.bfloat16), "tx", scatter_dimension=1, tiled=True)
    coefs = complex_times(owned, leaf_factor).astype(jnp.bfloat16)
    box_index = lax.axis_index("box")
    sources = lax.dynamic_slice_in_dim(slot_box, box_index * box_dev, box_dev)
    piece = lax.all_gather(coefs, "box", axis=0, tiled=True)
    count = piece.shape[0]
    taker = (sources[:, None] == jnp.arange(count, dtype=jnp.int32)[None, :]).astype(jnp.bfloat16)
    current = jnp.einsum("sn,nrk->srk", taker, piece, preferred_element_type=jnp.float32).astype(
        jnp.bfloat16
    )
    levels = self_factor.shape[0]
    local_bits = box_dev.bit_length() - 1
    for level in range(levels):
        if level < local_bits:
            span = 1 << level
            shaped = current.reshape(
                box_dev // (2 * span), 2, span, current.shape[1], current.shape[2]
            )
            partner = jnp.flip(shaped, axis=1).reshape(current.shape)
        else:
            partner = partner_2(current, "box", level - local_bits)
        mixed = complex_times(current, self_factor[level]) + complex_times(
            partner, cross_factor[level]
        )
        current = mixed.astype(jnp.bfloat16)
    return complex_times(current, target_factor).astype(jnp.bfloat16)


def solution(mesh):
    in_specs = (
        P("box", "tx", None),
        P(),
        P(),
        P("box", None, None),
        P(None, "box", None, None),
        P(None, "box", None, None),
        P("box", None, None),
    )
    out_specs = P("box", "tx", None)
    return jax.shard_map(
        per_device, mesh=mesh, in_specs=in_specs, out_specs=out_specs, check_vma=False
    )
```

profile of v0, /device:TPU:0, one launch (start us, length us, event | category | flops | bytes accessed | tf_op | source)
XLA Modules:
  0.0 153.6 jit_solution(15288603705547300182)
XLA Ops:
  6.5 0.8 broadcast_subtract_fusion
  7.3 6.3 %convert_bitcast_fusion = bf16[16,64,1024]{2,1,0:T(8,128)(2,1)} fusion(bf16[16,256,1024]{2,1,0:T(8,128)(2,1)} %param.7, s32[64]{0:T(128)S(1)} %broadcast_subtract_fusion), kind=kOutput, calls=%fused_computation.7 | convolution fusion | flops 537935872 | bytes 10486016 | tf_op jit(solution)/shard_map/pj,bju->bpu/dot_general | solution.py:39
  13.8 32.2 %reduce-scatter.2.cloned.1.call-done = bf16[16,16,1024]{2,1,0:T(8,128)(2,1)} async-done(((bf16[16,64,1024]{2,1,0:T(8,128)(2,1)}), bf16[16,16,1024]{2,1,0:T(8,128)(2,1)}) %reduce-scatter.2.cloned.1.call-update) | async-done | bytes 524304 | tf_op jit(solution)/shard_map/reduce_scatter | solution.py:40
  46.0 1.4 fusion.7
  47.4 0.4 fusion.9
  47.9 0.7 pad_maximum_fusion.1
  48.7 0.8 dynamic_slice.3
  49.4 43.1 %all-gather.2.cloned.1.call-done = bf16[512,16,128]{2,1,0:T(8,128)(2,1)} async-done(((bf16[16,16,128]{2,1,0:T(8,128)(2,1)}), bf16[512,16,128]{2,1,0:T(8,128)(2,1)}) %all-gather.2.cloned.1.call-update) | async-done | bytes 2097168 | tf_op jit(solution)/shard_map/all_gather | solution.py:44
  92.6 2.0 %fusion.4 = bf16[16,16,128]{2,0,1:T(8,128)(2,1)S(1)} fusion(bf16[512,16,128]{2,1,0:T(8,128)(2,1)} %all-gather.2.cloned.1.call-done, s32[16]{0:T(128)S(1)} %dynamic_slice.3), kind=kOutput, calls=%fused_computation.8 | convolution fusion | flops 33595392 | bytes 2162752 | tf_op jit(solution)/shard_map/sn,nrk->srk/dot_general | solution.py:47
  94.6 0.3 rev.16
  94.9 1.2 fusion.75
  96.1 1.1 fusion.77
  97.4 1.1 fusion.81
  98.5 1.1 fusion.79
  99.6 0.2 slice_subtract_fusion.17
  100.1 1.2 fusion.67
  101.3 1.1 fusion.69
  102.5 1.2 fusion.71
  103.7 1.1 fusion.73
  104.8 0.1 slice_subtract_fusion.15
  105.4 1.2 fusion.59
  106.6 1.1 fusion.61
  107.7 1.2 fusion.63
  109.0 1.1 fusion.65
  110.1 0.1 slice_subtract_fusion.13
  110.7 1.3 fusion.51
  112.1 1.1 fusion.53
  113.2 1.4 fusion.55
  114.6 1.1 fusion.57
  115.7 0.1 slice_subtract_fusion.11
  116.1 0.3 collective-permute-start
  116.5 0.2 fusion.47
  116.7 0.2 fusion.49
  117.0 0.4 collective-permute-done
  117.5 0.2 fusion.43
  117.7 0.2 fusion.45
  118.2 1.3 collective-permute-start.1
  119.5 0.2 fusion.39
  119.7 0.2 fusion.41
  120.0 2.5 %collective-permute-done.1 = bf16[16,16,128]{2,1,0:T(8,128)(2,1)S(1)} collective-permute-done((bf16[16,16,128]{2,1,0:T(8,128)(2,1)S(1)}, bf16[16,16,128]{2,1,0:T(8,128)(2,1)S(1)}, u32[]{:S(2)}, u32[]{:S(2)}) %collective-permute-start.1) | collective-permute-done | bytes 65568 | tf_op jit(solution)/shard_map/ppermute | solution.py:14
  122.5 0.2 fusion.35
  122.8 0.2 fusion.37
  123.3 2.4 %collective-permute-start.2 = (bf16[16,16,128]{2,1,0:T(8,128)(2,1)S(1)}, bf16[16,16,128]{2,1,0:T(8,128)(2,1)S(1)}, u32[]{:S(2)}, u32[]{:S(2)}) collective-permute-start(bf16[16,16,128]{2,1,0:T(8,128)(2,1)S(1)} %fusion.129), channel_id=1, source_target_pairs={{0,16},{16,0},{4,20},{20,4},{8,24},{24,8},{12,28},{28,12},{32,48},... | collective-permute-start | bytes 196616 | tf_op jit(solution)/shard_map/ppermute | solution.py:14
  125.6 0.2 fusion.31
  125.9 0.2 fusion.33
  126.2 2.9 %collective-permute-done.2 = bf16[16,16,128]{2,1,0:T(8,128)(2,1)S(1)} collective-permute-done((bf16[16,16,128]{2,1,0:T(8,128)(2,1)S(1)}, bf16[16,16,128]{2,1,0:T(8,128)(2,1)S(1)}, u32[]{:S(2)}, u32[]{:S(2)}) %collective-permute-start.2) | collective-permute-done | bytes 65568 | tf_op jit(solution)/shard_map/ppermute | solution.py:14
  129.1 0.2 fusion.27
  129.4 0.2 fusion.29
  129.9 1.3 collective-permute-start.3
  131.1 0.2 fusion.23
  131.4 0.2 fusion.25
  131.7 2.5 %collective-permute-done.3 = bf16[16,16,128]{2,1,0:T(8,128)(2,1)S(1)} collective-permute-done((bf16[16,16,128]{2,1,0:T(8,128)(2,1)S(1)}, bf16[16,16,128]{2,1,0:T(8,128)(2,1)S(1)}, u32[]{:S(2)}, u32[]{:S(2)}) %collective-permute-start.3) | collective-permute-done | bytes 65568 | tf_op jit(solution)/shard_map/ppermute | solution.py:14
  134.2 0.2 fusion.19
  134.5 0.2 fusion.21
  134.9 2.7 %collective-permute-start.4 = (bf16[16,16,128]{2,1,0:T(8,128)(2,1)S(1)}, bf16[16,16,128]{2,1,0:T(8,128)(2,1)S(1)}, u32[]{:S(2)}, u32[]{:S(2)}) collective-permute-start(bf16[16,16,128]{2,1,0:T(8,128)(2,1)S(1)} %fusion.131), channel_id=1, source_target_pairs={{0,64},{64,0},{4,68},{68,4},{8,72},{72,8},{12,76},{76,12},{16,80},... | collective-permute-start | bytes 196616 | tf_op jit(solution)/shard_map/ppermute | solution.py:14
  137.6 0.2 fusion.15
  137.9 0.2 fusion.17
  138.2 2.8 %collective-permute-done.4 = bf16[16,16,128]{2,1,0:T(8,128)(2,1)S(1)} collective-permute-done((bf16[16,16,128]{2,1,0:T(8,128)(2,1)S(1)}, bf16[16,16,128]{2,1,0:T(8,128)(2,1)S(1)}, u32[]{:S(2)}, u32[]{:S(2)}) %collective-permute-start.4) | collective-permute-done | bytes 65568 | tf_op jit(solution)/shard_map/ppermute | solution.py:14
  141.0 0.2 fusion.11
  141.2 0.2 fusion.13
  141.7 1.3 fusion.133
  143.0 1.2 fusion.135
  144.2 1.1 fusion.1
  145.3 1.5 pad_maximum_fusion
  (48 shorter events, 3.8 us)
Async XLA Ops:
  6.5 39.4 %copy-start = (bf16[16,512,128]{2,1,0:T(8,128)(2,1)S(1)}, bf16[16,512,128]{2,1,0:T(8,128)(2,1)}, u32[]{:S(2)}) copy-start(bf16[16,512,128]{2,1,0:T(8,128)(2,1)} %param.10) | copy-start | bytes 6291460
  6.5 39.4 %reduce-scatter.2.cloned.1.call-start = ((), (), s32[]{:S(2)}) async-start(), calls=%async_computation.1 | async-start | bytes 2621440 | tf_op jit(solution)/shard_map/reduce_scatter | solution.py:40
  13.7 78.9 %all-gather.2.cloned.1.call-start = ((), (), s32[]{:S(2)}) async-start(), calls=%async_computation.2 | async-start | bytes 2162688 | tf_op jit(solution)/shard_map/all_gather | solution.py:44
  46.0 1.4 copy-start.3
  110.7 5.8 %copy-start.1 = (bf16[9,16,64,128]{3,2,1,0:T(8,128)(2,1)S(1)}, bf16[9,16,64,128]{3,2,1,0:T(8,128)(2,1)}, u32[]{:S(2)}) copy-start(bf16[9,16,64,128]{3,2,1,0:T(8,128)(2,1)} %param.11) | copy-start | bytes 7077892
  113.2 4.3 %copy-start.2 = (bf16[9,16,64,128]{3,2,1,0:T(8,128)(2,1)S(1)}, bf16[9,16,64,128]{3,2,1,0:T(8,128)(2,1)}, u32[]{:S(2)}) copy-start(bf16[9,16,64,128]{3,2,1,0:T(8,128)(2,1)} %param.12) | copy-start | bytes 7077892
  116.1 1.3 collective-permute-start
  118.2 4.3 %collective-permute-start.1 = (bf16[16,16,128]{2,1,0:T(8,128)(2,1)S(1)}, bf16[16,16,128]{2,1,0:T(8,128)(2,1)S(1)}, u32[]{:S(2)}, u32[]{:S(2)}) collective-permute-start(bf16[16,16,128]{2,1,0:T(8,128)(2,1)S(1)} %fusion.128), channel_id=1, source_target_pairs={{0,8},{8,0},{4,12},{12,4},{16,24},{24,16},{20,28},{28,20},{32,40},... | collective-permute-start | bytes 196616 | tf_op jit(solution)/shard_map/ppermute | solution.py:14
  119.9 21.8 %slice-start = ((s8[8388608]{0:T(1024)(128)(4,1)}), s8[4194304]{0:T(1024)(128)(4,1)S(1)}, s32[]{:S(2)}) async-start(s8[8388608]{0:T(1024)(128)(4,1)} %bitcast.120), calls=%async_computation.3 | async-start | bytes 8388608
  123.3 5.8 %collective-permute-start.2 = (bf16[16,16,128]{2,1,0:T(8,128)(2,1)S(1)}, bf16[16,16,128]{2,1,0:T(8,128)(2,1)S(1)}, u32[]{:S(2)}, u32[]{:S(2)}) collective-permute-start(bf16[16,16,128]{2,1,0:T(8,128)(2,1)S(1)} %fusion.129), channel_id=1, source_target_pairs={{0,16},{16,0},{4,20},{20,4},{8,24},{24,8},{12,28},{28,12},{32,48},... | collective-permute-start | bytes 196616 | tf_op jit(solution)/shard_map/ppermute | solution.py:14
  129.8 11.9 %slice-start.1 = ((s8[8388608]{0:T(1024)(128)(4,1)}), s8[4194304]{0:T(1024)(128)(4,1)S(1)}, s32[]{:S(2)}) async-start(s8[8388608]{0:T(1024)(128)(4,1)} %bitcast.120), calls=%async_computation.4 | async-start | bytes 8388608
  129.9 4.3 %collective-permute-start.3 = (bf16[16,16,128]{2,1,0:T(8,128)(2,1)S(1)}, bf16[16,16,128]{2,1,0:T(8,128)(2,1)S(1)}, u32[]{:S(2)}, u32[]{:S(2)}) collective-permute-start(bf16[16,16,128]{2,1,0:T(8,128)(2,1)S(1)} %fusion.130), channel_id=1, source_target_pairs={{0,32},{32,0},{4,36},{36,4},{8,40},{40,8},{12,44},{44,12},{16,48},... | collective-permute-start | bytes 196616 | tf_op jit(solution)/shard_map/ppermute | solution.py:14
  134.9 6.0 %collective-permute-start.4 = (bf16[16,16,128]{2,1,0:T(8,128)(2,1)S(1)}, bf16[16,16,128]{2,1,0:T(8,128)(2,1)S(1)}, u32[]{:S(2)}, u32[]{:S(2)}) collective-permute-start(bf16[16,16,128]{2,1,0:T(8,128)(2,1)S(1)} %fusion.131), channel_id=1, source_target_pairs={{0,64},{64,0},{4,68},{68,4},{8,72},{72,8},{12,76},{76,12},{16,80},... | collective-permute-start | bytes 196616 | tf_op jit(solution)/shard_map/ppermute | solution.py:14
Sparse Core Ops, SparseCore 0:
  13.8 32.0 reduce-scatter.1
  48.8 43.7 all-gather.1
where the time goes:
time: 154 us
  waiting for transfers between devices  86.4 us (56%)
  matrix products  35.8 us (23%)
  between operations  13.9 us (9%)
  other arithmetic  8.3 us (5%)
  starting transfers between devices  7.97 us (5%)
    all_gather x1, waiting for transfers between devices, per_device(): piece = lax.all_gather(coefs, 'box', axis=0, tiled=True)  43.1 us
    reduce_scatter x1, waiting for transfers between devices, per_device(): lax.psum_scatter(picked.astype(jnp.bfloat16), 'tx', scatter_dimension=1,...  32.2 us
    dot_general x20, matrix products, complex_times(): jnp.einsum('brn,bnk->brk', values[..., inner:], matrix, preferred_element...  15 us
    dot_general x20, matrix products, complex_times(): jnp.einsum('brn,bnk->brk', values[..., :inner], matrix, preferred_element...  12.5 us
    ppermute x5, waiting for transfers between devices, partner_2(): return lax.ppermute(block, axis, route)  11 us
    ppermute x5, starting transfers between devices, partner_2(): return lax.ppermute(block, axis, route)  7.93 us
    dot_general x1, matrix products, per_device(): jnp.einsum('pj,bju->bpu', chooser, bank, preferred_element_type=jnp.float32)  6.33 us
  transfers between devices with their start and end apart: 7, of which 7 were waited for; matrix products, arithmetic and copies ran while one was open for 2% of the time, Pallas kernels for 0%

commit v1 on v0

v1 whole, which is shorter than its diff:
```python
import functools

import jax
import jax.numpy as jnp
from jax import lax
from jax.experimental import pallas as pl
from jax.experimental.pallas import tpu as pltpu
from jax.sharding import PartitionSpec as P

MESH = pl.DeviceIdType.MESH
GROUPS = 4


def half_routes():
    routes = {}
    for half, (first, second) in enumerate((("z", "y"), ("y", "z"))):
        unit = {"y": (1, 0), "z": (0, 1)}
        e1, e2 = unit[first], unit[second]
        at = lambda i, j: (i * e1[0] + j * e2[0], i * e1[1] + j * e2[1])
        base = half * 8
        full, low, high = (base, 8), (base, 4), (base + 4, 4)
        routes[half, "T1L"] = (at(-1, 0), full, first, -1)
        routes[half, "T1R"] = (at(1, 0), full, first, 1)
        routes[half, "T2L"] = (at(2, 0), low, first, -1)
        routes[half, "T2R"] = (at(2, 0), high, first, 1)
        for i in (0, -1, 1, 2):
            routes[half, "U1L", i] = (at(i, -1), full, second, -1)
            routes[half, "U1R", i] = (at(i, 1), full, second, 1)
            routes[half, "U2L", i] = (at(i, 2), low, second, -1)
            routes[half, "U2R", i] = (at(i, 2), high, second, 1)
    return routes


ROUTES = half_routes()
ROUTE_ID = {name: i for i, name in enumerate(ROUTES)}


def gather_levels_kernel(
    pick_ref, slot_ref, bank_ref, leaf_ref, self_ref, cross_ref, out_ref,
    bank_buf, leaf_buf, weights, part_send, part_recv, pool, core_send, core_recv, state, partner,
    bank_sem, leaf_sem, weight_sem, part_ssem, part_rsem, pool_ssem, pool_rsem,
    core_ssem, core_rsem, level_ssem, level_rsem,
):
    boxes = bank_ref.shape[0]
    stored = bank_ref.shape[1]
    columns = pick_ref.shape[0]
    own_cols = columns // 4
    levels = self_ref.shape[0]
    me = lax.axis_index("box")
    tx = lax.axis_index("tx")
    y = me // 8
    z = (me // 2) % 4
    core = me % 2

    def box_at(yy, zz, cc):
        return yy * 8 + zz * 2 + cc

    def chip_at(dy, dz):
        return ((y + dy + 4) % 4) * 4 + (z + dz + 4) % 4

    def device_at(dy, dz):
        return box_at((y + dy + 4) % 4, (z + dz + 4) % 4, core), tx

    core_mate = (box_at(y, z, 1 - core), tx)
    mates = [
        core_mate,
        (box_at(y, z + 1 - 2 * (z % 2), core), tx),
        device_at(0, 2),
        (box_at(y + 1 - 2 * (y % 2), z, core), tx),
        device_at(2, 0),
    ]
    tx_mates = [(me, (tx + d) % 4) for d in (1, 2, 3)]

    bank_in = [pltpu.make_async_copy(bank_ref.at[b], bank_buf.at[b], bank_sem.at[b]) for b in range(boxes)]
    leaf_in = [
        pltpu.make_async_copy(leaf_ref.at[pl.ds(4 * g, 4)], leaf_buf.at[pl.ds(4 * g, 4)], leaf_sem.at[g])
        for g in range(boxes // 4)
    ]
    for g in range(boxes // 4):
        leaf_in[g].start()
        for b in range(4 * g, 4 * g + 4):
            bank_in[b].start()
    weights_in = []
    for l in range(levels):
        weights_in.append((
            pltpu.make_async_copy(self_ref.at[l], weights.at[l, :, pl.ds(0, 64), :], weight_sem.at[l, 0]),
            pltpu.make_async_copy(cross_ref.at[l], weights.at[l, :, pl.ds(64, 64), :], weight_sem.at[l, 1]),
        ))
        for copy in weights_in[-1]:
            copy.start()

    barrier = pltpu.get_barrier_semaphore()
    greeted = tx_mates + [device_at(0, 1), device_at(0, 3), device_at(1, 0), device_at(3, 0),
                          device_at(0, 2), device_at(2, 0), core_mate]
    for dev in greeted:
        pl.semaphore_signal(barrier, inc=1, device_id=dev, device_id_type=MESH)

    lane = lax.broadcasted_iota(jnp.int32, (8, stored), 1)
    row = lax.broadcasted_iota(jnp.int32, (8, stored), 0)
    tiles = []
    for g in range(columns // 8):
        want = jnp.full((8, stored), -1, jnp.int32)
        for i in range(8):
            want = jnp.where(row == i, pick_ref[8 * g + i] - tx * stored, want)
        tiles.append(jnp.where(want == lane, 1.0, 0.0).astype(jnp.float32))
    chooser = jnp.concatenate(tiles, axis=0).astype(jnp.bfloat16)

    def turned(r, rows):
        lanes = lax.broadcasted_iota(jnp.int32, (rows, 128), 1)
        second = pltpu.roll(r[rows:], 64, axis=1)
        return r[:rows] + jnp.where(lanes < 64, -second, second)

    def leaf_of(b):
        chosen = jnp.dot(chooser, bank_buf[b], preferred_element_type=jnp.float32).astype(jnp.bfloat16)
        half = chosen.shape[1] // 2
        both = jnp.concatenate([chosen[:, :half], chosen[:, half:]], axis=0)
        r = jnp.dot(both, leaf_buf[b], preferred_element_type=jnp.float32)
        coefs = turned(r, columns).astype(jnp.bfloat16)
        for t in range(4):
            part_send[t, b] = coefs[t * own_cols:(t + 1) * own_cols]

    def part_copy(h, d):
        to = (tx + d) % 4
        return pltpu.make_async_remote_copy(
            part_send.at[to, pl.ds(8 * h, 8)], part_recv.at[d - 1, pl.ds(8 * h, 8)],
            part_ssem.at[h, d - 1], part_rsem.at[h, d - 1],
            device_id=(me, to), device_id_type=MESH)

    for g in range(boxes // 4):
        leaf_in[g].wait()
        for b in range(4 * g, 4 * g + 4):
            bank_in[b].wait()
        for b in range(4 * g, 4 * g + 4):
            leaf_of(b)
        if g == 1:
            pl.semaphore_wait(barrier, len(greeted))
        if g % 2 == 1:
            for d in (1, 3, 2):
                part_copy(g // 2, d).start()

    def route_copy(name, sending):
        (dy, dz), (first, count), axis, side = ROUTES[name]
        step = (side, 0) if axis == "y" else (0, side)
        if sending:
            item = (dy - step[0], dz - step[1])
            dev = device_at(-step[0], -step[1])
        else:
            item = (dy, dz)
            dev = device_at(step[0], step[1])
        start = chip_at(item[0], item[1]) * boxes + first
        where = pool.at[pl.ds(start, count)]
        k = ROUTE_ID[name]
        return pltpu.make_async_remote_copy(
            where, where, pool_ssem.at[k], pool_rsem.at[k], device_id=dev, device_id_type=MESH)

    def send(*names):
        for name in names:
            route_copy(name, True).start()

    def arrived(name):
        route_copy(name, False).wait_recv()

    mine = chip_at(0, 0) * boxes
    for h in (0, 1):
        for d in (1, 3, 2):
            part_copy(h, d).wait_recv()
        total = part_send[tx, pl.ds(8 * h, 8)].astype(jnp.float32)
        for d in range(3):
            total = total + part_recv[d, pl.ds(8 * h, 8)].astype(jnp.float32)
        pool[pl.ds(mine + 8 * h, 8)] = total.astype(jnp.bfloat16)
        send((h, "T1L"), (h, "T1R"), (h, "U1L", 0), (h, "U1R", 0))
    for h in (0, 1):
        arrived((h, "T1L"))
        send((h, "T2L"), (h, "U1L", -1), (h, "U1R", -1))
        arrived((h, "T1R"))
        send((h, "T2R"), (h, "U1L", 1), (h, "U1R", 1))
    for h in (0, 1):
        arrived((h, "U1L", 0))
        send((h, "U2L", 0))
        arrived((h, "U1R", 0))
        send((h, "U2R", 0))
    for h in (0, 1):
        arrived((h, "T2L"))
        arrived((h, "T2R"))
        send((h, "U1L", 2), (h, "U1R", 2))
    for i in (-1, 1, 2):
        for h in (0, 1):
            arrived((h, "U1L", i))
            send((h, "U2L", i))
            arrived((h, "U1R", i))
            send((h, "U2R", i))
    for i in (0, -1, 1, 2):
        for h in (0, 1):
            arrived((h, "U2L", i))
            arrived((h, "U2R", i))

    def chosen_box(slot):
        box = slot_ref[slot]
        dev = lax.shift_right_logical(box, 4)
        at = lax.shift_right_logical(dev, 1) * boxes + jnp.bitwise_and(box, 15)
        here = jnp.where(jnp.bitwise_and(dev, 1) == core, 1.0, 0.0).astype(jnp.float32)
        return pool[at].astype(jnp.float32) * here

    for s in range(boxes):
        core_send[s] = chosen_box(core_mate[0] * boxes + s).astype(jnp.bfloat16)
    core_copy = pltpu.make_async_remote_copy(
        core_send, core_recv, core_ssem, core_rsem, device_id=core_mate, device_id_type=MESH)
    core_copy.start()
    own = [chosen_box(me * boxes + s) for s in range(boxes)]
    core_copy.wait_recv()
    for s in range(boxes):
        state[0, s] = (own[s] + core_recv[s].astype(jnp.float32)).astype(jnp.bfloat16)

    local = boxes.bit_length() - 1
    per = boxes // GROUPS

    def level_copy(l, g):
        k = (l - local) * GROUPS + g
        return pltpu.make_async_remote_copy(
            state.at[l, pl.ds(per * g, per)], partner.at[l - local, pl.ds(per * g, per)],
            level_ssem.at[k], level_rsem.at[k], device_id=mates[l - local], device_id_type=MESH)

    lanes = lax.broadcasted_iota(jnp.int32, (own_cols, 128), 1)
    for l in range(levels):
        for copy in weights_in[l]:
            copy.wait()
        for g in range(GROUPS):
            if l >= local:
                level_copy(l, g).wait_recv()
            for s in range(per * g, per * g + per):
                a = state[l, s].astype(jnp.float32)
                b = (state[l, s ^ (1 << l)] if l < local else partner[l - local, s]).astype(jnp.float32)
                real = jnp.where(lanes < 64, a, pltpu.roll(b, 64, axis=1))
                imag = jnp.where(lanes < 64, pltpu.roll(a, 64, axis=1), b)
                both = jnp.concatenate([real, imag], axis=0).astype(jnp.bfloat16)
                r = jnp.dot(both, weights[l, s], preferred_element_type=jnp.float32)
                new = turned(r, own_cols).astype(jnp.bfloat16)
                if l + 1 < levels:
                    state[l + 1, s] = new
                else:
                    out_ref[s] = new
            if local <= l + 1 < levels:
                level_copy(l + 1, g).start()

    for h in (0, 1):
        for d in (1, 2, 3):
            part_copy(h, d).wait_send()
    for name in ROUTES:
        route_copy(name, True).wait_send()
    core_copy.wait_send()
    for l in range(local, levels):
        for g in range(GROUPS):
            level_copy(l, g).wait_send()


def gather_levels(pick, slot_box, bank, leaf_factor, self_factor, cross_factor):
    boxes, stored, width = bank.shape
    levels = self_factor.shape[0]
    cols = pick.shape[0] // 4
    bf16 = jnp.bfloat16
    dma = pltpu.SemaphoreType.DMA
    anyspace = pl.BlockSpec(memory_space=pltpu.HBM)
    smem = pl.BlockSpec(memory_space=pltpu.SMEM)
    local = boxes.bit_length() - 1
    return pl.pallas_call(
        gather_levels_kernel,
        out_shape=jax.ShapeDtypeStruct((boxes, cols, 128), bf16),
        in_specs=[smem, smem, anyspace, anyspace, anyspace, anyspace],
        out_specs=pl.BlockSpec(memory_space=pltpu.VMEM),
        scratch_shapes=[
            pltpu.VMEM((boxes, stored, width), bf16),
            pltpu.VMEM(leaf_factor.shape, bf16),
            pltpu.VMEM((levels, boxes, 128, 128), bf16),
            pltpu.VMEM((4, boxes, cols, 128), bf16),
            pltpu.VMEM((3, boxes, cols, 128), bf16),
            pltpu.VMEM((16 * boxes, cols, 128), bf16),
            pltpu.VMEM((boxes, cols, 128), bf16),
            pltpu.VMEM((boxes, cols, 128), bf16),
            pltpu.VMEM((levels, boxes, cols, 128), bf16),
            pltpu.VMEM((levels - local, boxes, cols, 128), bf16),
            dma((boxes,)), dma((boxes // 4,)), dma((levels, 2)),
            dma((2, 3)), dma((2, 3)), dma((len(ROUTES),)), dma((len(ROUTES),)),
            dma, dma, dma(((levels - local) * GROUPS,)), dma(((levels - local) * GROUPS,)),
        ],
        compiler_params=pltpu.CompilerParams(
            collective_id=0, has_side_effects=True, vmem_limit_bytes=36 << 20),
        name="gather_levels",
    )(pick, slot_box, bank, leaf_factor, self_factor, cross_factor)


def target_kernel(x_ref, t_ref, o_ref):
    for s in range(x_ref.shape[0]):
        x = x_ref[s].astype(jnp.float32)
        both = jnp.concatenate([x, pltpu.roll(x, 64, axis=1)], axis=0)[:, :64].astype(jnp.bfloat16)
        rows = x.shape[0]
        half = t_ref.shape[2] // 2
        r = jnp.dot(both, t_ref[s], preferred_element_type=jnp.float32)
        o_ref[s, :, :half] = (r[:rows, :half] - r[rows:, half:]).astype(jnp.bfloat16)
        o_ref[s, :, half:] = (r[:rows, half:] + r[rows:, :half]).astype(jnp.bfloat16)


def target_map(x, target_factor):
    boxes, cols, _ = x.shape
    k, width = target_factor.shape[1:]
    step = 4
    return pl.pallas_call(
        target_kernel,
        out_shape=jax.ShapeDtypeStruct((boxes, cols, width), jnp.bfloat16),
        grid=(boxes // step,),
        in_specs=[
            pl.BlockSpec((step, cols, 128), lambda i: (i, 0, 0)),
            pl.BlockSpec((step, k, width), lambda i: (i, 0, 0)),
        ],
        out_specs=pl.BlockSpec((step, cols, width), lambda i: (i, 0, 0)),
        compiler_params=pltpu.CompilerParams(vmem_limit_bytes=16 << 20),
        name="target_map",
    )(x, target_factor)


def per_device(bank, pick, slot_box, leaf_factor, self_factor, cross_factor, target_factor):
    x = gather_levels(pick, slot_box, bank, leaf_factor, self_factor, cross_factor)
    return target_map(x, target_factor)


def solution(mesh):
    in_specs = (
        P("box", "tx", None),
        P(),
        P(),
        P("box", None, None),
        P(None, "box", None, None),
        P(None, "box", None, None),
        P("box", None, None),
    )
    out_specs = P("box", "tx", None)
    return jax.shard_map(
        per_device, mesh=mesh, in_specs=in_specs, out_specs=out_specs, check_vma=False
    )
```

time: 154 us -> 62.3 us (0.40)
  waiting for transfers between devices: 86.4 us -> 0 us
  Pallas kernels: 0 us -> 52.4 us
  matrix products: 35.8 us -> 0 us
  between operations: 13.9 us -> 0.02 us
  local copies, waits for them, and re-layouts: 1.22 us -> 9.64 us
  other arithmetic: 8.3 us -> 0 us
  starting transfers between devices: 7.97 us -> 0 us
    pallas_call x0 -> x2, Pallas kernels: none -> 52.4 us  [the longest x1 49.3 us: gather_levels(): pl.pallas_call(gather_levels_kernel, out_shape=jax.ShapeDtypeStruct((boxe...]
    all_gather x1 -> x0, waiting for transfers between devices: 43.1 us -> none  [per_device(): piece = lax.all_gather(coefs, 'box', axis=0, tiled=True)]
    dot_general x42 -> x0, matrix products: 35.8 us -> none  [the longest x20 15 us: complex_times(): jnp.einsum('brn,bnk->brk', values[..., inner:], matrix, preferred_element...]
    reduce_scatter x1 -> x0, waiting for transfers between devices: 32.2 us -> none  [per_device(): lax.psum_scatter(picked.astype(jnp.bfloat16), 'tx', scatter_dimension=1,...]
    ppermute x5 -> x0, waiting for transfers between devices: 11 us -> none  [partner_2(): return lax.ppermute(block, axis, route)]
    unnamed x12 -> x14, local copies, waits for them, and re-layouts: 0.03 us -> 9.64 us
    ppermute x5 -> x0, starting transfers between devices: 7.93 us -> none  [partner_2(): return lax.ppermute(block, axis, route)]
    sub x18 -> x0, other arithmetic: 3.24 us -> none  [the longest x17 2.43 us: complex_times(): first[..., :half] - second[..., half:]]
  transfers between devices with their start and end apart: 7 -> 0, of which waited for: 7 -> 0; matrix products, arithmetic and copies ran while one was open for 2% -> 0% of each run, Pallas kernels for 0% -> 0%
where the time goes in v1:
time: 62.3 us; the launch traced here: 62.1 us
  Pallas kernels  52.4 us (84%)
  local copies, waits for them, and re-layouts  9.64 us (15%)
    pallas_call x1, Pallas kernels, gather_levels(): pl.pallas_call(gather_levels_kernel, out_shape=jax.ShapeDtypeStruct((boxe...  49.3 us
    unnamed x14, local copies, waits for them, and re-layouts  9.64 us
    pallas_call x1, Pallas kernels, target_map(): pl.pallas_call(target_kernel, out_shape=jax.ShapeDtypeStruct((boxes, cols...  3.08 us

profile of v1, /device:TPU:0, one launch (start us, length us, event | category | flops | bytes accessed | tf_op | source)
XLA Modules:
  0.0 62.1 jit_solution(14666831199655206982)
XLA Ops:
  0.0 0.0 copy-start.1
  0.0 3.4 %copy-done.1 = bf16[16,256,1024]{2,1,0:T(8,128)(2,1)S(1)} copy-done((bf16[16,256,1024]{2,1,0:T(8,128)(2,1)S(1)}, bf16[16,256,1024]{2,1,0:T(8,128)(2,1)}, u32[]{:S(2)}) %copy-start.1) | copy-done | bytes 8388632
  3.4 0.0 copy-start.2
  3.4 1.7 %copy-done.2 = bf16[9,16,64,128]{3,2,1,0:T(8,128)(2,1)S(1)} copy-done((bf16[9,16,64,128]{3,2,1,0:T(8,128)(2,1)S(1)}, bf16[9,16,64,128]{3,2,1,0:T(8,128)(2,1)}, u32[]{:S(2)}) %copy-start.2) | copy-done | bytes 2359320
  5.0 0.0 copy-start.3
  5.1 1.7 %copy-done.3 = bf16[9,16,64,128]{3,2,1,0:T(8,128)(2,1)S(1)} copy-done((bf16[9,16,64,128]{3,2,1,0:T(8,128)(2,1)S(1)}, bf16[9,16,64,128]{3,2,1,0:T(8,128)(2,1)}, u32[]{:S(2)}) %copy-start.3) | copy-done | bytes 2359320
  6.7 0.0 copy-start.4
  6.7 1.6 %copy-done.4 = bf16[16,512,128]{2,1,0:T(8,128)(2,1)S(1)} copy-done((bf16[16,512,128]{2,1,0:T(8,128)(2,1)S(1)}, bf16[16,512,128]{2,1,0:T(8,128)(2,1)}, u32[]{:S(2)}) %copy-start.4) | copy-done | bytes 2097176
  8.3 0.0 copy-start.5
  8.3 0.7 %copy-done.5 = s32[512]{0:T(512)S(1)} copy-done((s32[512]{0:T(512)S(1)}, s32[512]{0:T(512)}, u32[]{:S(2)}) %copy-start.5) | copy-done | bytes 2072
  9.0 0.0 copy-start.6
  9.0 0.7 %copy-done.6 = s32[64]{0:T(128)S(1)} copy-done((s32[64]{0:T(128)S(1)}, s32[64]{0:T(128)}, u32[]{:S(2)}) %copy-start.6) | copy-done | bytes 280
  9.6 0.0 copy-start
  9.6 49.3 %gather_levels.1.x_ref = bf16[16,16,128]{2,1,0:T(8,128)(2,1)S(1)} custom-call(s32[64]{0:T(128)S(1)} %copy-done.6, s32[512]{0:T(512)S(1)} %copy-done.5, bf16[16,256,1024]{2,1,0:T(8,128)(2,1)S(1)} %copy-done.1, bf16[16,512,128]{2,1,0:T(8,128)(2,1)S(1)} %copy-done.4, bf16[9,16,64,128]{3,2,1,0:T(8,128)(2,1)S(1)} %copy-done.2, bf16[9,16,64,128]{3,2,1,0:T(8,128)(2,1)S(1)} %copy-done.3), custom_call_target="tpu_custom_call" | custom-call | tf_op jit(solution)/shard_map/gather_levels/pallas_call | solution.py:265
  59.0 0.0 copy-done
  59.0 3.1 %target_map.1 = bf16[16,16,4096]{2,1,0:T(8,128)(2,1)} custom-call(bf16[16,16,128]{2,1,0:T(8,128)(2,1)S(1)} %gather_levels.1.x_ref, bf16[16,64,4096]{2,1,0:T(8,128)(2,1)S(1)} %copy-done), custom_call_target="tpu_custom_call" | custom-call | tf_op jit(solution)/shard_map/target_map/pallas_call | solution.py:306
Async XLA Ops:
  0.0 3.4 %copy-start.1 = (bf16[16,256,1024]{2,1,0:T(8,128)(2,1)S(1)}, bf16[16,256,1024]{2,1,0:T(8,128)(2,1)}, u32[]{:S(2)}) copy-start(bf16[16,256,1024]{2,1,0:T(8,128)(2,1)} %bank_ref.1) | copy-start | bytes 25165828
  3.4 1.7 %copy-start.2 = (bf16[9,16,64,128]{3,2,1,0:T(8,128)(2,1)S(1)}, bf16[9,16,64,128]{3,2,1,0:T(8,128)(2,1)}, u32[]{:S(2)}) copy-start(bf16[9,16,64,128]{3,2,1,0:T(8,128)(2,1)} %self_ref.1) | copy-start | bytes 7077892
  5.0 1.7 %copy-start.3 = (bf16[9,16,64,128]{3,2,1,0:T(8,128)(2,1)S(1)}, bf16[9,16,64,128]{3,2,1,0:T(8,128)(2,1)}, u32[]{:S(2)}) copy-start(bf16[9,16,64,128]{3,2,1,0:T(8,128)(2,1)} %cross_ref.1) | copy-start | bytes 7077892
  6.7 1.6 %copy-start.4 = (bf16[16,512,128]{2,1,0:T(8,128)(2,1)S(1)}, bf16[16,512,128]{2,1,0:T(8,128)(2,1)}, u32[]{:S(2)}) copy-start(bf16[16,512,128]{2,1,0:T(8,128)(2,1)} %leaf_ref.1) | copy-start | bytes 6291460
  8.3 0.7 %copy-start.5 = (s32[512]{0:T(512)S(1)}, s32[512]{0:T(512)}, u32[]{:S(2)}) copy-start(s32[512]{0:T(512)} %slot_ref.1) | copy-start | bytes 6148
  9.0 0.7 %copy-start.6 = (s32[64]{0:T(128)S(1)}, s32[64]{0:T(128)}, u32[]{:S(2)}) copy-start(s32[64]{0:T(128)} %pick_ref.1) | copy-start | bytes 772
  9.6 49.3 %copy-start = (bf16[16,64,4096]{2,1,0:T(8,128)(2,1)S(1)}, bf16[16,64,4096]{2,1,0:T(8,128)(2,1)}, u32[]{:S(2)}) copy-start(bf16[16,64,4096]{2,1,0:T(8,128)(2,1)} %t_ref.1) | copy-start | bytes 25165828

commit v2 on v1

v2 whole, which is shorter than its diff:
```python
import functools

import jax
import jax.numpy as jnp
from jax import lax
from jax.experimental import pallas as pl
from jax.experimental.pallas import tpu as pltpu
from jax.sharding import PartitionSpec as P

MESH = pl.DeviceIdType.MESH
GROUPS = 4
CHUNKS = 4
VMEM_MIB = 54
SIDES = (2, 1, 3)


def coefs_kernel(
    pick_ref, slot_ref, bank_ref, leaf_ref, self_ref, cross_ref, out_ref,
    picks, slots, bank_buf, leaf_buf, weights, part_send, part_recv, pool, core_send, core_recv,
    state, partner,
    index_sem, bank_sem, leaf_sem, weight_sem, part_ssem, part_rsem, ring_ssem, ring_rsem, cross_ssem, cross_rsem,
    core_ssem, core_rsem, level_ssem, level_rsem,
):
    boxes, stored = bank_ref.shape[:2]
    columns = pick_ref.shape[0]
    own_cols = columns // 4
    levels = self_ref.shape[0]
    chunk = boxes // CHUNKS
    per = boxes // GROUPS
    local = boxes.bit_length() - 1
    me = lax.axis_index("box")
    tx = lax.axis_index("tx")
    y = me // 8
    z = (me // 2) % 4
    core = me % 2

    def chip_at(dy, dz):
        return ((y + dy) % 4) * 4 + (z + dz) % 4

    def device_at(dy, dz):
        return ((y + dy) % 4) * 8 + ((z + dz) % 4) * 2 + core, tx

    core_mate = (y * 8 + z * 2 + 1 - core, tx)
    mates = [
        core_mate,
        device_at(0, 1 + 2 * (z % 2)),
        device_at(0, 2),
        device_at(1 + 2 * (y % 2), 0),
        device_at(2, 0),
    ]

    barrier = pltpu.get_barrier_semaphore()
    greeted = ([(me, (tx + d) % 4) for d in SIDES] + [device_at(0, d) for d in SIDES]
               + [device_at(d, 0) for d in SIDES] + [core_mate])
    for dev in greeted:
        pl.semaphore_signal(barrier, inc=1, device_id=dev, device_id_type=MESH)

    index_in = [
        pltpu.make_async_copy(pick_ref, picks, index_sem.at[0]),
        pltpu.make_async_copy(slot_ref, slots, index_sem.at[1]),
    ]
    bank_in = [pltpu.make_async_copy(bank_ref.at[b], bank_buf.at[b], bank_sem.at[b]) for b in range(boxes)]
    leaf_in = [
        pltpu.make_async_copy(
            leaf_ref.at[pl.ds(chunk * g, chunk)], leaf_buf.at[pl.ds(chunk * g, chunk)], leaf_sem.at[g])
        for g in range(CHUNKS)
    ]
    weights_in = [
        (pltpu.make_async_copy(self_ref.at[l], weights.at[l, :, pl.ds(0, 64), :], weight_sem.at[l, 0]),
         pltpu.make_async_copy(cross_ref.at[l], weights.at[l, :, pl.ds(64, 64), :], weight_sem.at[l, 1]))
        for l in range(levels)
    ]
    for copy in index_in:
        copy.start()
    for g in range(CHUNKS):
        leaf_in[g].start()
        for b in range(chunk * g, chunk * g + chunk):
            bank_in[b].start()

    for copy in index_in:
        copy.wait()
    lane = lax.broadcasted_iota(jnp.int32, (8, stored), 1)
    row = lax.broadcasted_iota(jnp.int32, (8, stored), 0)
    tiles = []
    for g in range(columns // 8):
        want = jnp.full((8, stored), -1, jnp.int32)
        for i in range(8):
            want = jnp.where(row == i, picks[8 * g + i] - tx * stored, want)
        tiles.append(jnp.where(want == lane, 1.0, 0.0).astype(jnp.float32))
    chooser = jnp.concatenate(tiles, axis=0).astype(jnp.bfloat16)

    def turned(r, rows):
        lanes = lax.broadcasted_iota(jnp.int32, (rows, 128), 1)
        second = pltpu.roll(r[rows:], 64, axis=1)
        return r[:rows] + jnp.where(lanes < 64, -second, second)

    def leaf_of(b):
        chosen = jnp.dot(chooser, bank_buf[b], preferred_element_type=jnp.float32).astype(jnp.bfloat16)
        half = chosen.shape[1] // 2
        both = jnp.concatenate([chosen[:, :half], chosen[:, half:]], axis=0)
        r = jnp.dot(both, leaf_buf[b], preferred_element_type=jnp.float32)
        coefs = turned(r, columns).astype(jnp.bfloat16)
        for t in range(4):
            part_send[t, b] = coefs[t * own_cols:(t + 1) * own_cols]

    def part_copy(h, d):
        to = (tx + d) % 4
        return pltpu.make_async_remote_copy(
            part_send.at[to, pl.ds(chunk * h, chunk)], part_recv.at[d - 1, pl.ds(chunk * h, chunk)],
            part_ssem.at[h, d - 1], part_rsem.at[h, d - 1],
            device_id=(me, to), device_id_type=MESH)

    for h in range(CHUNKS):
        leaf_in[h].wait()
        for b in range(chunk * h, chunk * h + chunk):
            bank_in[b].wait()
        for b in range(chunk * h, chunk * h + chunk):
            leaf_of(b)
        if h == CHUNKS - 1:
            pl.semaphore_wait(barrier, len(greeted))
            for e in range(CHUNKS):
                for d in SIDES:
                    part_copy(e, d).start()
    for l in range(levels):
        for copy in weights_in[l]:
            copy.start()

    def along(h, i, k):
        return (k, i) if h % 2 else (i, k)

    def place(h, i, k):
        return pool.at[pl.ds(chip_at(*along(h, i, k)) * boxes + chunk * h, chunk)]

    def ring_copy(h, k, sending):
        where = place(h, 0, 0 if sending else 4 - k)
        return pltpu.make_async_remote_copy(
            where, where, ring_ssem.at[h, k - 1], ring_rsem.at[h, k - 1],
            device_id=device_at(*along(h, 0, k)), device_id_type=MESH)

    def cross_copy(h, j, k, sending):
        where = place(h, 0 if sending else 4 - k, j)
        return pltpu.make_async_remote_copy(
            where, where, cross_ssem.at[h, j, k - 1], cross_rsem.at[h, j, k - 1],
            device_id=device_at(*along(h, k, 0)), device_id_type=MESH)

    mine = chip_at(0, 0) * boxes
    for h in range(CHUNKS):
        for d in (1, 3, 2):
            part_copy(h, d).wait_recv()
        total = part_send[tx, pl.ds(chunk * h, chunk)].astype(jnp.float32)
        for d in range(3):
            total = total + part_recv[d, pl.ds(chunk * h, chunk)].astype(jnp.float32)
        pool[pl.ds(mine + chunk * h, chunk)] = total.astype(jnp.bfloat16)
        for k in SIDES:
            ring_copy(h, k, True).start()
        for k in SIDES:
            cross_copy(h, 0, k, True).start()
    for h in range(CHUNKS):
        for k in (1, 3, 2):
            ring_copy(h, k, False).wait_recv()
            for i in SIDES:
                cross_copy(h, 4 - k, i, True).start()
    for h in range(CHUNKS):
        for j in range(4):
            for k in SIDES:
                cross_copy(h, j, k, False).wait_recv()

    def chosen_box(slot):
        box = slots[slot]
        dev = lax.shift_right_logical(box, 4)
        at = lax.shift_right_logical(dev, 1) * boxes + jnp.bitwise_and(box, 15)
        here = jnp.where(jnp.bitwise_and(dev, 1) == core, 1.0, 0.0).astype(jnp.float32)
        return pool[at].astype(jnp.float32) * here

    for s in range(boxes):
        core_send[s] = chosen_box(core_mate[0] * boxes + s).astype(jnp.bfloat16)
    core_copy = pltpu.make_async_remote_copy(
        core_send, core_recv, core_ssem, core_rsem, device_id=core_mate, device_id_type=MESH)
    core_copy.start()
    own = [chosen_box(me * boxes + s) for s in range(boxes)]
    core_copy.wait_recv()
    for s in range(boxes):
        state[0, s] = (own[s] + core_recv[s].astype(jnp.float32)).astype(jnp.bfloat16)

    lanes = lax.broadcasted_iota(jnp.int32, (own_cols, 128), 1)

    def mixed(a, b, w):
        a, b = a.astype(jnp.float32), b.astype(jnp.float32)
        real = jnp.where(lanes < 64, a, pltpu.roll(b, 64, axis=1))
        imag = jnp.where(lanes < 64, pltpu.roll(a, 64, axis=1), b)
        both = jnp.concatenate([real, imag], axis=0).astype(jnp.bfloat16)
        r = jnp.dot(both, w, preferred_element_type=jnp.float32)
        return turned(r, own_cols).astype(jnp.bfloat16)

    def level_copy(l, g):
        part = pl.ds(per * g, per)
        return pltpu.make_async_remote_copy(
            state.at[l, part], partner.at[l - local, part],
            level_ssem.at[l - local, g], level_rsem.at[l - local, g], device_id=mates[l - local], device_id_type=MESH)

    for l in range(levels):
        for copy in weights_in[l]:
            copy.wait()
        for g in range(GROUPS):
            if l >= local:
                level_copy(l, g).wait_recv()
            for s in range(per * g, per * g + per):
                other = state[l, s ^ (1 << l)] if l < local else partner[l - local, s]
                new = mixed(state[l, s], other, weights[l, s])
                if l + 1 < levels:
                    state[l + 1, s] = new
                else:
                    out_ref[s] = new
            if local <= l + 1 < levels:
                level_copy(l + 1, g).start()

    for h in range(CHUNKS):
        for d in (1, 2, 3):
            part_copy(h, d).wait_send()
            ring_copy(h, d, True).wait_send()
            for j in range(4):
                cross_copy(h, j, d, True).wait_send()
    core_copy.wait_send()
    for l in range(local, levels):
        for g in range(GROUPS):
            level_copy(l, g).wait_send()


def coefs_of_device(pick, slot_box, bank, leaf_factor, self_factor, cross_factor):
    boxes = bank.shape[0]
    levels = self_factor.shape[0]
    cols = pick.shape[0] // 4
    crossing = levels - boxes.bit_length() + 1
    bf16 = jnp.bfloat16
    dma = pltpu.SemaphoreType.DMA
    hbm = pl.BlockSpec(memory_space=pltpu.HBM)
    tiles = lambda *lead: pltpu.VMEM((*lead, cols, 128), bf16)
    pair = lambda *shape: [dma(shape), dma(shape)]
    return pl.pallas_call(
        coefs_kernel,
        out_shape=jax.ShapeDtypeStruct((boxes, cols, 128), bf16),
        in_specs=[hbm] * 6,
        out_specs=pl.BlockSpec(memory_space=pltpu.VMEM),
        scratch_shapes=[
            pltpu.SMEM(pick.shape, jnp.int32),
            pltpu.SMEM(slot_box.shape, jnp.int32),
            pltpu.VMEM(bank.shape, bf16),
            pltpu.VMEM(leaf_factor.shape, bf16),
            pltpu.VMEM((levels, boxes, 128, 128), bf16),
            tiles(4, boxes), tiles(3, boxes), tiles(16 * boxes), tiles(boxes), tiles(boxes),
            tiles(levels, boxes), tiles(crossing, boxes),
            dma((2,)), dma((boxes,)), dma((CHUNKS,)), dma((levels, 2)),
            *pair(CHUNKS, 3), *pair(CHUNKS, 3), *pair(CHUNKS, 4, 3), dma, dma, *pair(crossing, GROUPS),
        ],
        compiler_params=pltpu.CompilerParams(
            collective_id=0, has_side_effects=True, vmem_limit_bytes=VMEM_MIB << 20),
        name="coefs",
    )(pick, slot_box, bank, leaf_factor, self_factor, cross_factor)


def target_kernel(x_ref, t_ref, o_ref):
    for s in range(x_ref.shape[0]):
        x = x_ref[s].astype(jnp.float32)
        both = jnp.concatenate([x, pltpu.roll(x, 64, axis=1)], axis=0)[:, :64].astype(jnp.bfloat16)
        rows = x.shape[0]
        half = t_ref.shape[2] // 2
        r = jnp.dot(both, t_ref[s], preferred_element_type=jnp.float32)
        o_ref[s, :, :half] = (r[:rows, :half] - r[rows:, half:]).astype(jnp.bfloat16)
        o_ref[s, :, half:] = (r[:rows, half:] + r[rows:, :half]).astype(jnp.bfloat16)


def target_map(x, target_factor):
    boxes, cols, _ = x.shape
    k, width = target_factor.shape[1:]
    step = 4
    return pl.pallas_call(
        target_kernel,
        out_shape=jax.ShapeDtypeStruct((boxes, cols, width), jnp.bfloat16),
        grid=(boxes // step,),
        in_specs=[
            pl.BlockSpec((step, cols, 128), lambda i: (i, 0, 0)),
            pl.BlockSpec((step, k, width), lambda i: (i, 0, 0)),
        ],
        out_specs=pl.BlockSpec((step, cols, width), lambda i: (i, 0, 0)),
        compiler_params=pltpu.CompilerParams(vmem_limit_bytes=16 << 20),
        name="target_map",
    )(x, target_factor)


def per_device(bank, pick, slot_box, leaf_factor, self_factor, cross_factor, target_factor):
    x = coefs_of_device(pick, slot_box, bank, leaf_factor, self_factor, cross_factor)
    return target_map(x, target_factor)


def solution(mesh):
    in_specs = (
        P("box", "tx", None),
        P(),
        P(),
        P("box", None, None),
        P(None, "box", None, None),
        P(None, "box", None, None),
        P("box", None, None),
    )
    out_specs = P("box", "tx", None)
    return jax.shard_map(
        per_device, mesh=mesh, in_specs=in_specs, out_specs=out_specs, check_vma=False
    )
```

time: 62.3 us -> 51.2 us (0.82)
  local copies, waits for them, and re-layouts: 9.64 us -> 0.84 us
  Pallas kernels: 52.4 us -> 50.2 us
    unnamed x14 -> x4, local copies, waits for them, and re-layouts: 9.64 us -> 0.84 us
    pallas_call x1, Pallas kernels: 49.3 us -> 47.1 us  [coefs_of_device(): pl.pallas_call(coefs_kernel, out_shape=jax.ShapeDtypeStruct((boxes, cols,...]
where the time goes in v2:
time: 51.2 us; the launch traced here: 51.1 us
  Pallas kernels  50.2 us (98%)
  local copies, waits for them, and re-layouts  0.84 us (2%)
    pallas_call x1, Pallas kernels, coefs_of_device(): pl.pallas_call(coefs_kernel, out_shape=jax.ShapeDtypeStruct((boxes, cols,...  47.1 us
    pallas_call x1, Pallas kernels, target_map(): pl.pallas_call(target_kernel, out_shape=jax.ShapeDtypeStruct((boxes, cols...  3.07 us

profile of v2, /device:TPU:0, one launch (start us, length us, event | category | flops | bytes accessed | tf_op | source)
XLA Modules:
  0.0 51.1 jit_solution(17106280465726299637)
XLA Ops:
  0.0 0.0 copy-start
  0.0 47.1 %coefs.1.x_ref = bf16[16,16,128]{2,1,0:T(8,128)(2,1)} custom-call(s32[64]{0:T(128)} %pick_ref.1, s32[512]{0:T(512)} %slot_ref.1, bf16[16,256,1024]{2,1,0:T(8,128)(2,1)} %bank_ref.1, bf16[16,512,128]{2,1,0:T(8,128)(2,1)} %leaf_ref.1, bf16[9,16,64,128]{3,2,1,0:T(8,128)(2,1)} %self_ref.1, bf16[9,16,64,128]{3,2,1,0:T(8,128)(2,1)} %cross_ref.1), custom_call_target="tpu_custom_call" | custom-call | tf_op jit(solution)/shard_map/coefs/pallas_call | solution.py:239
  47.1 0.0 copy-done
  47.1 0.0 copy-start.1
  47.2 0.8 %copy-done.1 = bf16[16,16,128]{2,1,0:T(8,128)(2,1)S(1)} copy-done((bf16[16,16,128]{2,1,0:T(8,128)(2,1)S(1)}, bf16[16,16,128]{2,1,0:T(8,128)(2,1)}, u32[]{:S(2)}) %copy-start.1) | copy-done | bytes 65560
  48.0 3.1 %target_map.1 = bf16[16,16,4096]{2,1,0:T(8,128)(2,1)} custom-call(bf16[16,16,128]{2,1,0:T(8,128)(2,1)S(1)} %copy-done.1, bf16[16,64,4096]{2,1,0:T(8,128)(2,1)S(1)} %copy-done), custom_call_target="tpu_custom_call" | custom-call | tf_op jit(solution)/shard_map/target_map/pallas_call | solution.py:276
Async XLA Ops:
  0.0 47.1 %copy-start = (bf16[16,64,4096]{2,1,0:T(8,128)(2,1)S(1)}, bf16[16,64,4096]{2,1,0:T(8,128)(2,1)}, u32[]{:S(2)}) copy-start(bf16[16,64,4096]{2,1,0:T(8,128)(2,1)} %t_ref.1) | copy-start | bytes 25165828
  47.1 0.8 %copy-start.1 = (bf16[16,16,128]{2,1,0:T(8,128)(2,1)S(1)}, bf16[16,16,128]{2,1,0:T(8,128)(2,1)}, u32[]{:S(2)}) copy-start(bf16[16,16,128]{2,1,0:T(8,128)(2,1)} %coefs.1.x_ref) | copy-start | bytes 196612

commit v3 on v2

--- a/solution.py
+++ b/solution.py
@@ -18,7 +18,7 @@
     pick_ref, slot_ref, bank_ref, leaf_ref, self_ref, cross_ref, out_ref,
     picks, slots, bank_buf, leaf_buf, weights, part_send, part_recv, pool, core_send, core_recv,
     state, partner,
-    index_sem, bank_sem, leaf_sem, weight_sem, part_ssem, part_rsem, ring_ssem, ring_rsem, cross_ssem, cross_rsem,
+    index_sem, bank_sem, leaf_sem, weight_sem, part_ssem, part_rsem, pool_ssem, ring_rsem, cross_rsem,
     core_ssem, core_rsem, level_ssem, level_rsem,
 ):
     boxes, stored = bank_ref.shape[:2]
@@ -59,23 +59,23 @@
         pltpu.make_async_copy(pick_ref, picks, index_sem.at[0]),
         pltpu.make_async_copy(slot_ref, slots, index_sem.at[1]),
     ]
-    bank_in = [pltpu.make_async_copy(bank_ref.at[b], bank_buf.at[b], bank_sem.at[b]) for b in range(boxes)]
-    leaf_in = [
-        pltpu.make_async_copy(
-            leaf_ref.at[pl.ds(chunk * g, chunk)], leaf_buf.at[pl.ds(chunk * g, chunk)], leaf_sem.at[g])
-        for g in range(CHUNKS)
+    bank_in, leaf_in = [[
+        pltpu.make_async_copy(ref.at[pl.ds(chunk * h, chunk)], buf.at[pl.ds(chunk * h, chunk)], sem.at[h])
+        for h in range(CHUNKS)
+    ] for ref, buf, sem in ((bank_ref, bank_buf, bank_sem), (leaf_ref, leaf_buf, leaf_sem))]
+    weights_in = [
+        pltpu.make_async_copy(ref, weights.at[:, :, pl.ds(128 * i, 64), :], weight_sem.at[i])
+        for i, ref in enumerate((self_ref, cross_ref))
     ]
-    weights_in = [
-        (pltpu.make_async_copy(self_ref.at[l], weights.at[l, :, pl.ds(0, 64), :], weight_sem.at[l, 0]),
-         pltpu.make_async_copy(cross_ref.at[l], weights.at[l, :, pl.ds(64, 64), :], weight_sem.at[l, 1]))
-        for l in range(levels)
-    ]
+
+    def fetch(h):
+        leaf_in[h].start()
+        bank_in[h].start()
+
     for copy in index_in:
         copy.start()
-    for g in range(CHUNKS):
-        leaf_in[g].start()
-        for b in range(chunk * g, chunk * g + chunk):
-            bank_in[b].start()
+    fetch(0)
+    fetch(1)
 
     for copy in index_in:
         copy.wait()
@@ -107,13 +107,16 @@
         to = (tx + d) % 4
         return pltpu.make_async_remote_copy(
             part_send.at[to, pl.ds(chunk * h, chunk)], part_recv.at[d - 1, pl.ds(chunk * h, chunk)],
-            part_ssem.at[h, d - 1], part_rsem.at[h, d - 1],
+            part_ssem, part_rsem.at[h],
             device_id=(me, to), device_id_type=MESH)
 
     for h in range(CHUNKS):
         leaf_in[h].wait()
-        for b in range(chunk * h, chunk * h + chunk):
-            bank_in[b].wait()
+        bank_in[h].wait()
+        if h + 2 < CHUNKS:
+            fetch(h + 2)
+        else:
+            weights_in[h + 2 - CHUNKS].start()
         for b in range(chunk * h, chunk * h + chunk):
             leaf_of(b)
         if h == CHUNKS - 1:
@@ -121,9 +124,25 @@
             for e in range(CHUNKS):
                 for d in SIDES:
                     part_copy(e, d).start()
-    for l in range(levels):
-        for copy in weights_in[l]:
-            copy.start()
+
+    for copy in weights_in:
+        copy.wait()
+    side = lax.broadcasted_iota(jnp.int32, (64, 128), 1) < 64
+
+    def widen(l, s):
+        for i in (0, 128):
+            m = weights[l, s, i:i + 64].astype(jnp.float32)
+            m = pltpu.roll(m, 64, axis=1)
+            weights[l, s, i + 64:i + 128] = jnp.where(side, -m, m).astype(jnp.bfloat16)
+
+    def widen_level(l, carry):
+        def some(i, carry):
+            for s in range(4):
+                widen(l, 4 * i + s)
+            return carry
+        return lax.fori_loop(0, boxes // 4, some, carry)
+
+    lax.fori_loop(0, local, widen_level, 0)
 
     def along(h, i, k):
         return (k, i) if h % 2 else (i, k)
@@ -134,36 +153,37 @@
     def ring_copy(h, k, sending):
         where = place(h, 0, 0 if sending else 4 - k)
         return pltpu.make_async_remote_copy(
-            where, where, ring_ssem.at[h, k - 1], ring_rsem.at[h, k - 1],
+            where, where, pool_ssem, ring_rsem.at[h, k - 1],
             device_id=device_at(*along(h, 0, k)), device_id_type=MESH)
 
     def cross_copy(h, j, k, sending):
         where = place(h, 0 if sending else 4 - k, j)
         return pltpu.make_async_remote_copy(
-            where, where, cross_ssem.at[h, j, k - 1], cross_rsem.at[h, j, k - 1],
+            where, where, pool_ssem, cross_rsem,
             device_id=device_at(*along(h, k, 0)), device_id_type=MESH)
 
     mine = chip_at(0, 0) * boxes
     for h in range(CHUNKS):
-        for d in (1, 3, 2):
-            part_copy(h, d).wait_recv()
+        whole = part_recv.at[:, pl.ds(chunk * h, chunk)]
+        pltpu.make_async_copy(whole, whole, part_rsem.at[h]).wait()
         total = part_send[tx, pl.ds(chunk * h, chunk)].astype(jnp.float32)
         for d in range(3):
             total = total + part_recv[d, pl.ds(chunk * h, chunk)].astype(jnp.float32)
         pool[pl.ds(mine + chunk * h, chunk)] = total.astype(jnp.bfloat16)
         for k in SIDES:
             ring_copy(h, k, True).start()
-        for k in SIDES:
-            cross_copy(h, 0, k, True).start()
+        if h % 2:
+            for e in (h - 1, h):
+                for k in SIDES:
+                    cross_copy(e, 0, k, True).start()
     for h in range(CHUNKS):
         for k in (1, 3, 2):
             ring_copy(h, k, False).wait_recv()
             for i in SIDES:
                 cross_copy(h, 4 - k, i, True).start()
-    for h in range(CHUNKS):
-        for j in range(4):
-            for k in SIDES:
-                cross_copy(h, j, k, False).wait_recv()
+    lax.fori_loop(local, levels, widen_level, 0)
+    crossed = pool.at[pl.ds(0, 12 * boxes)]
+    pltpu.make_async_copy(crossed, crossed, cross_rsem).wait()
 
     def chosen_box(slot):
         box = slots[slot]
@@ -182,31 +202,23 @@
     for s in range(boxes):
         state[0, s] = (own[s] + core_recv[s].astype(jnp.float32)).astype(jnp.bfloat16)
 
-    lanes = lax.broadcasted_iota(jnp.int32, (own_cols, 128), 1)
-
-    def mixed(a, b, w):
-        a, b = a.astype(jnp.float32), b.astype(jnp.float32)
-        real = jnp.where(lanes < 64, a, pltpu.roll(b, 64, axis=1))
-        imag = jnp.where(lanes < 64, pltpu.roll(a, 64, axis=1), b)
-        both = jnp.concatenate([real, imag], axis=0).astype(jnp.bfloat16)
-        r = jnp.dot(both, w, preferred_element_type=jnp.float32)
-        return turned(r, own_cols).astype(jnp.bfloat16)
-
     def level_copy(l, g):
         part = pl.ds(per * g, per)
         return pltpu.make_async_remote_copy(
             state.at[l, part], partner.at[l - local, part],
-            level_ssem.at[l - local, g], level_rsem.at[l - local, g], device_id=mates[l - local], device_id_type=MESH)
+            level_ssem, level_rsem.at[l - local, g], device_id=mates[l - local], device_id_type=MESH)
+
+    def product(x, l, s, i):
+        return jnp.dot(x, weights[l, s, i:i + 128], preferred_element_type=jnp.float32)
 
     for l in range(levels):
-        for copy in weights_in[l]:
-            copy.wait()
+        mine_part = [product(state[l, s], l, s, 0) for s in range(boxes)]
         for g in range(GROUPS):
             if l >= local:
                 level_copy(l, g).wait_recv()
             for s in range(per * g, per * g + per):
                 other = state[l, s ^ (1 << l)] if l < local else partner[l - local, s]
-                new = mixed(state[l, s], other, weights[l, s])
+                new = (mine_part[s] + product(other, l, s, 128)).astype(jnp.bfloat16)
                 if l + 1 < levels:
                     state[l + 1, s] = new
                 else:
@@ -214,16 +226,11 @@
             if local <= l + 1 < levels:
                 level_copy(l + 1, g).start()
 
-    for h in range(CHUNKS):
-        for d in (1, 2, 3):
-            part_copy(h, d).wait_send()
-            ring_copy(h, d, True).wait_send()
-            for j in range(4):
-                cross_copy(h, j, d, True).wait_send()
+    pltpu.make_async_copy(part_recv, part_recv, part_ssem).wait()
+    sent = pool.at[pl.ds(0, 15 * boxes)]
+    pltpu.make_async_copy(sent, sent, pool_ssem).wait()
     core_copy.wait_send()
-    for l in range(local, levels):
-        for g in range(GROUPS):
-            level_copy(l, g).wait_send()
+    pltpu.make_async_copy(partner, partner, level_ssem).wait()
 
 
 def coefs_of_device(pick, slot_box, bank, leaf_factor, self_factor, cross_factor):
@@ -235,7 +242,6 @@
     dma = pltpu.SemaphoreType.DMA
     hbm = pl.BlockSpec(memory_space=pltpu.HBM)
     tiles = lambda *lead: pltpu.VMEM((*lead, cols, 128), bf16)
-    pair = lambda *shape: [dma(shape), dma(shape)]
     return pl.pallas_call(
         coefs_kernel,
         out_shape=jax.ShapeDtypeStruct((boxes, cols, 128), bf16),
@@ -246,11 +252,11 @@
             pltpu.SMEM(slot_box.shape, jnp.int32),
             pltpu.VMEM(bank.shape, bf16),
             pltpu.VMEM(leaf_factor.shape, bf16),
-            pltpu.VMEM((levels, boxes, 128, 128), bf16),
+            pltpu.VMEM((levels, boxes, 256, 128), bf16),
             tiles(4, boxes), tiles(3, boxes), tiles(16 * boxes), tiles(boxes), tiles(boxes),
             tiles(levels, boxes), tiles(crossing, boxes),
-            dma((2,)), dma((boxes,)), dma((CHUNKS,)), dma((levels, 2)),
-            *pair(CHUNKS, 3), *pair(CHUNKS, 3), *pair(CHUNKS, 4, 3), dma, dma, *pair(crossing, GROUPS),
+            dma((2,)), dma((CHUNKS,)), dma((CHUNKS,)), dma((2,)),
+            dma, dma((CHUNKS,)), dma, dma((CHUNKS, 3)), dma, dma, dma, dma, dma((crossing, GROUPS)),
         ],
         compiler_params=pltpu.CompilerParams(
             collective_id=0, has_side_effects=True, vmem_limit_bytes=VMEM_MIB << 20),

time: 51.2 us -> 46.8 us (0.914)
  Pallas kernels: 50.2 us -> 45.8 us
    pallas_call x1, Pallas kernels: 47.1 us -> 42.7 us  [coefs_of_device(): pl.pallas_call(coefs_kernel, out_shape=jax.ShapeDtypeStruct((boxes, cols,...]
where the time goes in v3:
time: 46.8 us; the launch traced here: 46.7 us
  Pallas kernels  45.8 us (98%)
  local copies, waits for them, and re-layouts  0.84 us (2%)
    pallas_call x1, Pallas kernels, coefs_of_device(): pl.pallas_call(coefs_kernel, out_shape=jax.ShapeDtypeStruct((boxes, cols,...  42.7 us
    pallas_call x1, Pallas kernels, target_map(): pl.pallas_call(target_kernel, out_shape=jax.ShapeDtypeStruct((boxes, cols...  3.06 us

profile of v3, /device:TPU:0, one launch (start us, length us, event | category | flops | bytes accessed | tf_op | source)
XLA Modules:
  0.0 46.7 jit_solution(7867830912699527385)
XLA Ops:
  0.0 0.0 copy-start
  0.0 42.7 %coefs.1.x_ref = bf16[16,16,128]{2,1,0:T(8,128)(2,1)} custom-call(s32[64]{0:T(128)} %pick_ref.1, s32[512]{0:T(512)} %slot_ref.1, bf16[16,256,1024]{2,1,0:T(8,128)(2,1)} %bank_ref.1, bf16[16,512,128]{2,1,0:T(8,128)(2,1)} %leaf_ref.1, bf16[9,16,64,128]{3,2,1,0:T(8,128)(2,1)} %self_ref.1, bf16[9,16,64,128]{3,2,1,0:T(8,128)(2,1)} %cross_ref.1), custom_call_target="tpu_custom_call" | custom-call | tf_op jit(solution)/shard_map/coefs/pallas_call | solution.py:245
  42.8 0.0 copy-done
  42.8 0.0 copy-start.1
  42.8 0.8 %copy-done.1 = bf16[16,16,128]{2,1,0:T(8,128)(2,1)S(1)} copy-done((bf16[16,16,128]{2,1,0:T(8,128)(2,1)S(1)}, bf16[16,16,128]{2,1,0:T(8,128)(2,1)}, u32[]{:S(2)}) %copy-start.1) | copy-done | bytes 65560
  43.6 3.1 %target_map.1 = bf16[16,16,4096]{2,1,0:T(8,128)(2,1)} custom-call(bf16[16,16,128]{2,1,0:T(8,128)(2,1)S(1)} %copy-done.1, bf16[16,64,4096]{2,1,0:T(8,128)(2,1)S(1)} %copy-done), custom_call_target="tpu_custom_call" | custom-call | tf_op jit(solution)/shard_map/target_map/pallas_call | solution.py:282
Async XLA Ops:
  0.0 42.8 %copy-start = (bf16[16,64,4096]{2,1,0:T(8,128)(2,1)S(1)}, bf16[16,64,4096]{2,1,0:T(8,128)(2,1)}, u32[]{:S(2)}) copy-start(bf16[16,64,4096]{2,1,0:T(8,128)(2,1)} %t_ref.1) | copy-start | bytes 25165828
  42.8 0.8 %copy-start.1 = (bf16[16,16,128]{2,1,0:T(8,128)(2,1)S(1)}, bf16[16,16,128]{2,1,0:T(8,128)(2,1)}, u32[]{:S(2)}) copy-start(bf16[16,16,128]{2,1,0:T(8,128)(2,1)} %coefs.1.x_ref) | copy-start | bytes 196612

commit v4 on v3

--- a/solution.py
+++ b/solution.py
@@ -119,11 +119,11 @@
             weights_in[h + 2 - CHUNKS].start()
         for b in range(chunk * h, chunk * h + chunk):
             leaf_of(b)
-        if h == CHUNKS - 1:
+        if h == 1:
             pl.semaphore_wait(barrier, len(greeted))
-            for e in range(CHUNKS):
-                for d in SIDES:
-                    part_copy(e, d).start()
+        for e in range(h + 1) if h == 1 else [h] if h > 1 else []:
+            for d in SIDES:
+                part_copy(e, d).start()
 
     for copy in weights_in:
         copy.wait()
@@ -172,10 +172,8 @@
         pool[pl.ds(mine + chunk * h, chunk)] = total.astype(jnp.bfloat16)
         for k in SIDES:
             ring_copy(h, k, True).start()
-        if h % 2:
-            for e in (h - 1, h):
-                for k in SIDES:
-                    cross_copy(e, 0, k, True).start()
+        for k in SIDES:
+            cross_copy(h, 0, k, True).start()
     for h in range(CHUNKS):
         for k in (1, 3, 2):
             ring_copy(h, k, False).wait_recv()
@@ -264,33 +262,56 @@
     )(pick, slot_box, bank, leaf_factor, self_factor, cross_factor)
 
 
-def target_kernel(x_ref, t_ref, o_ref):
-    for s in range(x_ref.shape[0]):
-        x = x_ref[s].astype(jnp.float32)
-        both = jnp.concatenate([x, pltpu.roll(x, 64, axis=1)], axis=0)[:, :64].astype(jnp.bfloat16)
-        rows = x.shape[0]
-        half = t_ref.shape[2] // 2
-        r = jnp.dot(both, t_ref[s], preferred_element_type=jnp.float32)
-        o_ref[s, :, :half] = (r[:rows, :half] - r[rows:, half:]).astype(jnp.bfloat16)
-        o_ref[s, :, half:] = (r[:rows, half:] + r[rows:, :half]).astype(jnp.bfloat16)
+def target_kernel(x_ref, t_ref, o_ref, buf, sem):
+    boxes, cols, _ = x_ref.shape
+    width = o_ref.shape[2] // 2
+    tile = 256
+    first = lax.broadcasted_iota(jnp.int32, (cols, 128), 1) < 64
+    copies = [
+        pltpu.make_async_copy(buf.at[pl.ds(4 * g, 4)], o_ref.at[pl.ds(4 * g, 4)], sem.at[g])
+        for g in range(boxes // 4)
+    ]
+    for g in range(boxes // 4):
+        rows = []
+        for i in range(4):
+            x = x_ref[4 * g + i].astype(jnp.float32)
+            swapped = pltpu.roll(x, 64, axis=1)
+            if i % 2 == 0:
+                pairs = [jnp.where(first, x, 0.0), jnp.where(first, swapped, 0.0)]
+            else:
+                pairs = [jnp.where(first, 0.0, swapped), jnp.where(first, 0.0, x)]
+            block = jnp.concatenate(pairs, axis=0)
+            none = jnp.zeros_like(block)
+            rows.append(jnp.concatenate([block, none] if i < 2 else [none, block], axis=1))
+        left = jnp.concatenate(rows, axis=0).astype(jnp.bfloat16)
+        part = slice(256 * g, 256 * g + 256)
+        for c in range(0, width, tile):
+            re, im = [
+                jnp.dot(left, t_ref[part, at:at + tile], preferred_element_type=jnp.float32)
+                for at in (c, width + c)
+            ]
+            for i in range(4):
+                a, b, e = 2 * cols * i, 2 * cols * i + cols, 2 * cols * i + 2 * cols
+                buf[4 * g + i, :, c:c + tile] = (re[a:b] - im[b:e]).astype(jnp.bfloat16)
+                buf[4 * g + i, :, width + c:width + c + tile] = (im[a:b] + re[b:e]).astype(jnp.bfloat16)
+        copies[g].start()
+    for copy in copies:
+        copy.wait()
 
 
 def target_map(x, target_factor):
     boxes, cols, _ = x.shape
     k, width = target_factor.shape[1:]
-    step = 4
+    vmem = pl.BlockSpec(memory_space=pltpu.VMEM)
     return pl.pallas_call(
         target_kernel,
         out_shape=jax.ShapeDtypeStruct((boxes, cols, width), jnp.bfloat16),
-        grid=(boxes // step,),
-        in_specs=[
-            pl.BlockSpec((step, cols, 128), lambda i: (i, 0, 0)),
-            pl.BlockSpec((step, k, width), lambda i: (i, 0, 0)),
-        ],
-        out_specs=pl.BlockSpec((step, cols, width), lambda i: (i, 0, 0)),
+        in_specs=[vmem, vmem],
+        out_specs=pl.BlockSpec(memory_space=pltpu.HBM),
+        scratch_shapes=[pltpu.VMEM((boxes, cols, width), jnp.bfloat16), pltpu.SemaphoreType.DMA((boxes // 4,))],
         compiler_params=pltpu.CompilerParams(vmem_limit_bytes=16 << 20),
         name="target_map",
-    )(x, target_factor)
+    )(x, target_factor.reshape(boxes * k, width))
 
 
 def per_device(bank, pick, slot_box, leaf_factor, self_factor, cross_factor, target_factor):

time: 46.8 us -> 43.7 us (0.934)
  Pallas kernels: 45.8 us -> 42.7 us
    pallas_call x1, Pallas kernels: 42.7 us -> 40.6 us  [coefs_of_device(): pl.pallas_call(coefs_kernel, out_shape=jax.ShapeDtypeStruct((boxes, cols,...]
    pallas_call x1, Pallas kernels: 3.06 us -> 2.13 us  [target_map(): pl.pallas_call(target_kernel, out_shape=jax.ShapeDtypeStruct((boxes, cols...]
where the time goes in v4:
time: 43.7 us; the launch traced here: 43.6 us
  Pallas kernels  42.7 us (98%)
  local copies, waits for them, and re-layouts  0.84 us (2%)
    pallas_call x1, Pallas kernels, coefs_of_device(): pl.pallas_call(coefs_kernel, out_shape=jax.ShapeDtypeStruct((boxes, cols,...  40.6 us
    pallas_call x1, Pallas kernels, target_map(): pl.pallas_call(target_kernel, out_shape=jax.ShapeDtypeStruct((boxes, cols...  2.13 us

profile of v4, /device:TPU:0, one launch (start us, length us, event | category | flops | bytes accessed | tf_op | source)
XLA Modules:
  0.0 43.6 jit_solution(18085114021830535332)
XLA Ops:
  0.0 0.0 copy-start
  0.0 40.6 %coefs.1.x_ref = bf16[16,16,128]{2,1,0:T(8,128)(2,1)} custom-call(s32[64]{0:T(128)} %pick_ref.1, s32[512]{0:T(512)} %slot_ref.1, bf16[16,256,1024]{2,1,0:T(8,128)(2,1)} %bank_ref.1, bf16[16,512,128]{2,1,0:T(8,128)(2,1)} %leaf_ref.1, bf16[9,16,64,128]{3,2,1,0:T(8,128)(2,1)} %self_ref.1, bf16[9,16,64,128]{3,2,1,0:T(8,128)(2,1)} %cross_ref.1), custom_call_target="tpu_custom_call" | custom-call | tf_op jit(solution)/shard_map/coefs/pallas_call | solution.py:243
  40.6 0.0 copy-done
  40.6 0.0 copy-start.1
  40.6 0.8 %copy-done.1 = bf16[16,16,128]{2,1,0:T(8,128)(2,1)S(1)} copy-done((bf16[16,16,128]{2,1,0:T(8,128)(2,1)S(1)}, bf16[16,16,128]{2,1,0:T(8,128)(2,1)}, u32[]{:S(2)}) %copy-start.1) | copy-done | bytes 65560
  41.4 2.1 %target_map.1 = bf16[16,16,4096]{2,1,0:T(8,128)(2,1)} custom-call(bf16[16,16,128]{2,1,0:T(8,128)(2,1)S(1)} %copy-done.1, bf16[1024,4096]{1,0:T(8,128)(2,1)S(1)} %bitcast.1), custom_call_target="tpu_custom_call" | custom-call | tf_op jit(solution)/shard_map/target_map/pallas_call | solution.py:306
Async XLA Ops:
  0.0 40.6 %copy-start = (bf16[16,64,4096]{2,1,0:T(8,128)(2,1)S(1)}, bf16[16,64,4096]{2,1,0:T(8,128)(2,1)}, u32[]{:S(2)}) copy-start(bf16[16,64,4096]{2,1,0:T(8,128)(2,1)} %param.13) | copy-start | bytes 25165828
  40.6 0.8 %copy-start.1 = (bf16[16,16,128]{2,1,0:T(8,128)(2,1)S(1)}, bf16[16,16,128]{2,1,0:T(8,128)(2,1)}, u32[]{:S(2)}) copy-start(bf16[16,16,128]{2,1,0:T(8,128)(2,1)} %coefs.1.x_ref) | copy-start | bytes 196612

commit v5 on v4

--- a/solution.py
+++ b/solution.py
@@ -76,6 +76,7 @@
         copy.start()
     fetch(0)
     fetch(1)
+    fetch(2)
 
     for copy in index_in:
         copy.wait()
@@ -113,9 +114,9 @@
     for h in range(CHUNKS):
         leaf_in[h].wait()
         bank_in[h].wait()
-        if h + 2 < CHUNKS:
-            fetch(h + 2)
-        else:
+        if h + 3 < CHUNKS:
+            fetch(h + 3)
+        elif h >= CHUNKS - 2:
             weights_in[h + 2 - CHUNKS].start()
         for b in range(chunk * h, chunk * h + chunk):
             leaf_of(b)
@@ -125,8 +126,6 @@
             for d in SIDES:
                 part_copy(e, d).start()
 
-    for copy in weights_in:
-        copy.wait()
     side = lax.broadcasted_iota(jnp.int32, (64, 128), 1) < 64
 
     def widen(l, s):
@@ -141,8 +140,6 @@
                 widen(l, 4 * i + s)
             return carry
         return lax.fori_loop(0, boxes // 4, some, carry)
-
-    lax.fori_loop(0, local, widen_level, 0)
 
     def along(h, i, k):
         return (k, i) if h % 2 else (i, k)
@@ -179,7 +176,9 @@
             ring_copy(h, k, False).wait_recv()
             for i in SIDES:
                 cross_copy(h, 4 - k, i, True).start()
-    lax.fori_loop(local, levels, widen_level, 0)
+    for copy in weights_in:
+        copy.wait()
+    lax.fori_loop(0, levels, widen_level, 0)
     crossed = pool.at[pl.ds(0, 12 * boxes)]
     pltpu.make_async_copy(crossed, crossed, cross_rsem).wait()
 

time: 43.7 us -> 43.9 us (level)
  no operation moved by 1% of the time
where the time goes in v5:
time: 43.9 us; the launch traced here: 43.8 us
  Pallas kernels  42.9 us (98%)
  local copies, waits for them, and re-layouts  0.84 us (2%)
    pallas_call x1, Pallas kernels, coefs_of_device(): pl.pallas_call(coefs_kernel, out_shape=jax.ShapeDtypeStruct((boxes, cols,...  40.8 us
    pallas_call x1, Pallas kernels, target_map(): pl.pallas_call(target_kernel, out_shape=jax.ShapeDtypeStruct((boxes, cols...  2.12 us

profile of v5, /device:TPU:0, one launch (start us, length us, event | category | flops | bytes accessed | tf_op | source)
XLA Modules:
  0.0 43.8 jit_solution(3231893633903789493)
XLA Ops:
  0.0 0.0 copy-start
  0.0 40.8 %coefs.1.x_ref = bf16[16,16,128]{2,1,0:T(8,128)(2,1)} custom-call(s32[64]{0:T(128)} %pick_ref.1, s32[512]{0:T(512)} %slot_ref.1, bf16[16,256,1024]{2,1,0:T(8,128)(2,1)} %bank_ref.1, bf16[16,512,128]{2,1,0:T(8,128)(2,1)} %leaf_ref.1, bf16[9,16,64,128]{3,2,1,0:T(8,128)(2,1)} %self_ref.1, bf16[9,16,64,128]{3,2,1,0:T(8,128)(2,1)} %cross_ref.1), custom_call_target="tpu_custom_call" | custom-call | tf_op jit(solution)/shard_map/coefs/pallas_call | solution.py:242
  40.8 0.0 copy-done
  40.8 0.0 copy-start.1
  40.8 0.8 %copy-done.1 = bf16[16,16,128]{2,1,0:T(8,128)(2,1)S(1)} copy-done((bf16[16,16,128]{2,1,0:T(8,128)(2,1)S(1)}, bf16[16,16,128]{2,1,0:T(8,128)(2,1)}, u32[]{:S(2)}) %copy-start.1) | copy-done | bytes 65560
  41.7 2.1 %target_map.1 = bf16[16,16,4096]{2,1,0:T(8,128)(2,1)} custom-call(bf16[16,16,128]{2,1,0:T(8,128)(2,1)S(1)} %copy-done.1, bf16[1024,4096]{1,0:T(8,128)(2,1)S(1)} %bitcast.1), custom_call_target="tpu_custom_call" | custom-call | tf_op jit(solution)/shard_map/target_map/pallas_call | solution.py:305
Async XLA Ops:
  0.0 40.8 %copy-start = (bf16[16,64,4096]{2,1,0:T(8,128)(2,1)S(1)}, bf16[16,64,4096]{2,1,0:T(8,128)(2,1)}, u32[]{:S(2)}) copy-start(bf16[16,64,4096]{2,1,0:T(8,128)(2,1)} %param.13) | copy-start | bytes 25165828
  40.8 0.8 %copy-start.1 = (bf16[16,16,128]{2,1,0:T(8,128)(2,1)S(1)}, bf16[16,16,128]{2,1,0:T(8,128)(2,1)}, u32[]{:S(2)}) copy-start(bf16[16,16,128]{2,1,0:T(8,128)(2,1)} %coefs.1.x_ref) | copy-start | bytes 196612
